TPU v7x, 32 devices: a whole 2x2x4 slice. The times are simulated.
32 devices in a mesh: gx: 8 (over z, x), gy: 4 (over y, core).
Axes of the slice: x: 2, y: 2, z: 4, core: 2. Of those that a mesh axis runs over, the one named last changes fastest.
Arguments:
- ensemble: float32 [16, 512, 1024], P('gx', None, 'gy'), may hold values from -6 to 6
- obs_values: float32 [4, 128], replicated, may hold values from -6 to 6
- obs_error: float32 [4, 128], replicated, may hold values from 0.3 to 3
- tile_weight: float32 [4, 128, 8, 4], P(None, None, 'gx', 'gy'), may hold values from 0.2 to 1
- owner_device: int32 [4], replicated, may hold values from 0 to 31
- obs_cells: int32 [4, 128], replicated, may hold values from 0 to 16383
Outputs:
- analysis_ensemble: float32 [16, 512, 1024], P('gx', None, 'gy')
Inputs may be any that keep to these rules, and one draw needn't show every extreme that they name: `owner_device`: device numbers count gy fastest: the device at index i of gx and j of gy is number i times the length of gy plus j. `obs_cells`: cell c of a tile lies c // 256 cells along the first direction and c % 256 along the second from the tile's first cell; cells may repeat.
All inputs are finite; a program needn't handle non-finite values.
Results may differ from a plain program's by a relative error of at most 0.00015.
Values sent between devices are 32-bit elements; how exact they have to be, the bound alone decides.
No kernel may reach another device: no remote copies, remote signals or barrier semaphores. Data moves between devices by JAX's collectives and lax.ppermute only.
A program may use at most 64 MiB of HBM per device.

v0:
```python
import functools

import jax
import jax.numpy as jnp
from jax import lax
from jax.experimental import pallas as pl
from jax.experimental.pallas import tpu as pltpu
from jax.sharding import PartitionSpec as P


EPSILON = 1e-06
IN_EIGHTHS = 4
OUT_EIGHTHS = 3
LIGHT = pltpu.CompilerParams(vmem_limit_bytes=16 << 20)
ROWS = 8
F32 = jnp.float32
BF16 = jnp.bfloat16
VMEM = pltpu.MemorySpace.VMEM
SMEM = pltpu.MemorySpace.SMEM


def split_two(value):
    high = value.astype(BF16)
    low = (value - high.astype(F32)).astype(BF16)
    return high, low


def pairs_of(batches):
    return [(b, later) for b in range(batches) for later in range(b + 1, batches)]


def pick_body(
    owner_in,
    cells_in,
    weight_in,
    ens_ref,
    blocks_ref,
    *refs,
    tile_rows,
    first,
    gx_count,
    gy_count,
):
    pieces = refs[:gx_count]
    window, payload_ref, owner_ref, cells_ref, weight_ref, in_sems, out_sems, small_sems = refs[
        gx_count:
    ]
    batches, nobs = cells_ref.shape
    held, _, cols = ens_ref.shape
    row_at = lax.axis_index("gx")
    col_at = lax.axis_index("gy")
    me = row_at * gy_count + col_at

    def fetch(tile):
        rows = pl.ds(tile * tile_rows, tile_rows)
        return pltpu.make_async_copy(ens_ref.at[:, rows, :], window.at[tile], in_sems.at[tile])

    def put(tile):
        other = window.at[tile, :, pl.ds(first, tile_rows - first), :]
        return pltpu.make_async_copy(other, blocks_ref.at[tile], out_sems.at[tile])

    small = [
        pltpu.make_async_copy(source, target, small_sems.at[at])
        for at, (source, target) in enumerate(
            [(owner_in, owner_ref), (cells_in, cells_ref), (weight_in, weight_ref)]
        )
    ]
    for copy in small:
        copy.start()
    for tile in range(gx_count):
        fetch(tile).start()
    payload_ref[...] = jnp.zeros_like(payload_ref)
    for copy in small:
        copy.wait()
    pairs_at = -(-held * batches // 8) * 8
    for at, (b, later) in enumerate(pairs_of(batches)):
        row = pairs_at + at
        payload_ref[row : row + 1, :] = jnp.where(owner_ref[later] == me, weight_ref[b : b + 1, :], 0.0)
    hits = []
    for b in range(batches):
        cell = cells_ref[b : b + 1, :]
        row_hit = (lax.broadcasted_iota(jnp.int32, (tile_rows, nobs), 0) == cell // cols).astype(F32)
        row_hit = row_hit.astype(BF16)
        col_hit = lax.broadcasted_iota(jnp.int32, (cols, nobs), 0) == cell % cols
        hits.append((jnp.concatenate([row_hit] * 3, axis=0), col_hit))
    for tile in range(gx_count):
        fetch(tile).wait()
    for tile in range(gx_count):
        put(tile).start()
    folds = cols // nobs
    for slot in range(gx_count):
        for m in range(held):
            for fold in range(folds):
                at = (m * folds + fold) * first
                lanes = slice(fold * nobs, (fold + 1) * nobs)
                pieces[slot][at : at + first, :] = window[row_at ^ slot, m, :first, lanes]
    for b in range(batches):
        row_hit, col_hit = hits[b]
        owner_row = owner_ref[b] // gy_count
        mine = owner_ref[b] % gy_count == col_at
        for m in range(held):
            values = window[owner_row, m]
            high = values.astype(BF16)
            rest = values - high.astype(F32)
            middle, low = split_two(rest)
            stacked = jnp.concatenate([high, middle, low], axis=0)
            columns = lax.dot_general(
                stacked, row_hit, (((0,), (0,)), ((), ())), preferred_element_type=F32
            )
            picked = jnp.sum(jnp.where(col_hit, columns, 0.0), axis=0, keepdims=True)
            row = m * batches + b
            payload_ref[row : row + 1, :] = jnp.where(mine, picked, 0.0)
    for slot in range(gx_count):
        pieces[slot][held * folds * first :, :] = payload_ref[...]
    for tile in range(gx_count):
        put(tile).wait()


def observed_at(owner_ref, cells_ref, b, tile_rows, tile_cols, gy_count, inverse):
    nobs = cells_ref.shape[1]
    cell = cells_ref[b : b + 1, :]
    owner = owner_ref[b]
    ox = ((owner // gy_count) * tile_rows + cell // tile_cols).astype(F32) * inverse
    oy = ((owner % gy_count) * tile_cols + cell % tile_cols).astype(F32) * inverse
    down_x = jnp.transpose(jnp.broadcast_to(ox, (nobs, nobs)))
    down_y = jnp.transpose(jnp.broadcast_to(oy, (nobs, nobs)))
    return ox, oy, down_x, down_y


def tables_body(
    owner_ref, cells_ref, x_ref, y_ref, taper_ref, *, tile_rows, tile_cols, gy_count, inverse
):
    batches, nobs = cells_ref.shape
    left = lax.axis_index("gy") * tile_cols
    places = [
        observed_at(owner_ref, cells_ref, b, tile_rows, tile_cols, gy_count, inverse)
        for b in range(batches)
    ]
    for b, (_, _, down_x, down_y) in enumerate(places):
        x_ref[b] = down_x
        for piece in range(tile_cols // nobs):
            lanes = slice(piece * nobs, (piece + 1) * nobs)
            grid = lax.broadcasted_iota(jnp.int32, (nobs, nobs), 1) + (left + piece * nobs)
            away = down_y - grid.astype(F32) * inverse
            y_ref[b, :, lanes] = away * away
    for at, (b, later) in enumerate(pairs_of(batches)):
        dx = places[b][2] - places[later][0]
        dy = places[b][3] - places[later][1]
        taper_ref[at] = pl.reciprocal(1.0 + (dx * dx + dy * dy))


def merge_body(*refs, base, picks):
    pieces, out_ref = refs[:-1], refs[-1]
    total = None
    for slot, piece in enumerate(pieces):
        out_ref[slot * picks : (slot + 1) * picks, :] = piece[base : base + picks, :]
        weights = piece[base + picks :, :]
        total = weights if total is None else total + weights
    out_ref[len(pieces) * picks :, :] = total


def factor_rows(increment):
    high, low = split_two(increment)
    return jnp.concatenate(
        [jnp.concatenate([high, high], axis=1), jnp.concatenate([low, low], axis=1)], axis=0
    )


def chain_body(
    values_ref, errors_ref, weight_ref, taper_ref, *refs, held, gx_count, gy_count
):
    batches, nobs = values_ref.shape
    members = held * gx_count
    parts, (a_ref, w_ref, prior_ref) = refs[:gy_count], refs[gy_count:]
    row_at = lax.axis_index("gx")
    picks = -(-held * batches // 8) * 8

    def total(first, count):
        rows = [part[first : first + count, :] for part in parts]
        return sum(rows[1:], rows[0])

    for slot in range(gx_count):
        part = total(slot * picks, picks)
        source = held * (row_at ^ slot)
        for m in range(held):
            for b in range(batches):
                row = m * batches + b
                prior_ref[b, pl.ds(source + m, 1), :] = part[row : row + 1, :]
    weights = total(gx_count * picks, parts[0].shape[0] - gx_count * picks)
    for b in range(batches):
        prior = prior_ref[b]
        average = jnp.mean(prior, axis=0, keepdims=True)
        anomaly = prior - average
        spread = jnp.sum(anomaly * anomaly, axis=0, keepdims=True) / (members - 1) + EPSILON
        scaled = anomaly / (spread * (members - 1))
        high, low = split_two(scaled)
        stacked = jnp.concatenate([high, high, low], axis=0).astype(F32)
        wide = a_ref.shape[2]
        if wide > stacked.shape[0]:
            stacked = jnp.concatenate(
                [stacked, jnp.zeros((wide - stacked.shape[0], nobs), F32)], axis=0
            )
        upright = jnp.transpose(stacked).astype(BF16)
        a_ref[b] = upright
        noise = errors_ref[b : b + 1, :]
        post_var = 1.0 / (1.0 / spread + 1.0 / noise)
        post_mean = post_var * (average / spread + values_ref[b : b + 1, :] / noise)
        increment = post_mean - average + (jnp.sqrt(post_var / spread) - 1.0) * anomaly
        w_ref[b] = factor_rows(increment * weight_ref[b : b + 1, :])
        for at, (earlier, later) in enumerate(pairs_of(batches)):
            if earlier != b:
                continue
            there = prior_ref[later]
            deviation = there - jnp.mean(there, axis=0, keepdims=True)
            high, low = split_two(deviation)
            covariance = jnp.dot(
                upright[:, : 3 * members],
                jnp.concatenate([high, low, high], axis=0),
                preferred_element_type=F32,
            )
            high, low = split_two(covariance * taper_ref[at])
            change = jnp.dot(
                factor_rows(increment * weights[at : at + 1, :]),
                jnp.concatenate([high, low], axis=0),
                preferred_element_type=F32,
            )
            prior_ref[later] = there + (change[:members] + change[members:])


def update_body(a_ref, w_ref, x_ref, y_ref, *refs, first, depth, tile_rows, parts, inverse):
    gx_count, ins, outs = parts
    pieces, others, targets = refs[:gx_count], refs[gx_count:ins], refs[ins : ins + outs]
    scratch = refs[-1]
    members, rows, cols = scratch.shape
    held = members // gx_count
    batches, nobs, _ = x_ref.shape
    row_at = lax.axis_index("gx")
    begin = first + pl.program_id(0) * rows
    top = row_at * tile_rows + begin
    from_ref, to_ref = scratch, targets[0]

    def unpack():
        for slot, piece in enumerate(pieces):
            for m in range(held):
                for fold in range(cols // nobs):
                    at = (m * (cols // nobs) + fold) * depth + begin
                    lanes = slice(fold * nobs, (fold + 1) * nobs)
                    from_ref[held * (row_at ^ slot) + m, :, lanes] = piece[
                        pl.ds(pl.multiple_of(at, ROWS), rows), :
                    ]

    if others:
        pl.when(begin < depth)(unpack)

        @pl.when(begin >= depth)
        def _():
            from_ref[...] = others[0][...]
    else:
        unpack()
    if len(targets) > 1:
        to_ref = scratch
    states = [from_ref[:, r, :] for r in range(rows)]
    for b in range(batches):
        scaled = a_ref[b][:, : 3 * members]
        increment = w_ref[b]
        for r in range(rows):
            state = states[r]
            deviation = state - jnp.mean(state, axis=0, keepdims=True)
            high, low = split_two(deviation)
            covariance = jnp.dot(
                scaled, jnp.concatenate([high, low, high], axis=0), preferred_element_type=F32
            )
            dx = x_ref[b] - (top + r).astype(F32) * inverse
            dx = 1.0 + dx * dx
            away = jnp.concatenate([dx] * (cols // nobs), axis=1) + y_ref[b]
            gain = covariance * pl.reciprocal(away)
            high, low = split_two(gain)
            change = jnp.dot(
                increment, jnp.concatenate([high, low], axis=0), preferred_element_type=F32
            )
            states[r] = state + (change[:members] + change[members:])
    for r in range(rows):
        to_ref[:, r, :] = states[r]
    if len(targets) > 1:
        for slot, target in enumerate(targets):
            target[...] = to_ref[pl.ds(held * (row_at ^ slot), held)]


def whole(array):
    return pl.BlockSpec(array.shape, lambda i: (0,) * array.ndim)


def update(pieces, others, tables, first, count, depth, tile_rows, cols, outs, inverse):
    gx_count = len(pieces)
    batches, nobs, _ = tables[2].shape
    members = tables[1].shape[1] // 2
    rows = count if not others else ROWS
    cells = count * cols * batches * nobs
    out = members // outs
    return pl.pallas_call(
        functools.partial(
            update_body,
            first=first,
            depth=depth,
            tile_rows=tile_rows,
            parts=(gx_count, gx_count + len(others), outs),
            inverse=inverse,
        ),
        grid=(count // rows,),
        in_specs=[whole(array) for array in (*tables, *pieces)]
        + [
            pl.BlockSpec(
                (members, rows, cols),
                lambda i: (0, jnp.maximum(i - (depth - first) // rows, 0), 0),
            )
        ]
        * len(others),
        out_specs=[pl.BlockSpec((out, rows, cols), lambda i: (0, i, 0))] * outs,
        out_shape=[jax.ShapeDtypeStruct((out, count, cols), F32)] * outs,
        scratch_shapes=[pltpu.VMEM((members, rows, cols), F32)],
        cost_estimate=pl.CostEstimate(
            flops=cells * members * 10,
            bytes_accessed=8 * members * count * cols,
            transcendentals=cells,
        ),
        compiler_params=LIGHT,
        name="update",
    )(*tables, *pieces, *others)


def assemble_body(whole_ref, *refs, first, tile_rows, here):
    pieces, out_ref, sems = refs[:-2], refs[-2], refs[-1]
    row_at = lax.axis_index("gx")
    copies = []
    for tile in range(whole_ref.shape[0]):
        rows = pl.ds(tile * tile_rows, first)
        copies.append(
            pltpu.make_async_copy(whole_ref.at[tile], out_ref.at[:, rows, :], sems.at[tile])
        )
    for slot, piece in enumerate(pieces):
        start = pl.multiple_of((row_at ^ slot) * tile_rows + first, here)
        rows = pl.ds(start, tile_rows - first)
        copies.append(
            pltpu.make_async_copy(
                piece, out_ref.at[:, rows, :], sems.at[whole_ref.shape[0] + slot]
            )
        )
    for copy in copies:
        copy.start()
    for copy in copies:
        copy.wait()


def local(ensemble, obs_values, obs_error, tile_weight, owner_device, obs_cells):
    gx_count = lax.axis_size("gx")
    gy_count = lax.axis_size("gy")
    held, all_rows, tile_cols = ensemble.shape
    members = held * gx_count
    tile_rows = all_rows // gx_count
    batches, nobs = obs_cells.shape
    first = tile_rows * IN_EIGHTHS // 8
    rest = tile_rows - first
    early = tile_rows * OUT_EIGHTHS // 8
    inverse = 1.0 / (all_rows // 4)
    weight = tile_weight[:, :, 0, 0]
    picks, pairs = [-(-n // 8) * 8 for n in (held * batches, len(pairs_of(batches)))]
    payload = picks + pairs
    state_rows = held * (tile_cols // nobs) * first
    in_smem = pl.BlockSpec(memory_space=SMEM)
    in_vmem = pl.BlockSpec(memory_space=VMEM)
    in_hbm = pl.BlockSpec(memory_space=pltpu.MemorySpace.HBM)
    geometry = dict(tile_rows=tile_rows, tile_cols=tile_cols, gy_count=gy_count, inverse=inverse)

    blocks, *pieces = pl.pallas_call(
        functools.partial(
            pick_body, tile_rows=tile_rows, first=first, gx_count=gx_count, gy_count=gy_count
        ),
        in_specs=[in_hbm] * 4,
        out_specs=[in_hbm] + [in_vmem] * gx_count,
        out_shape=[jax.ShapeDtypeStruct((gx_count, held, rest, tile_cols), F32)]
        + [jax.ShapeDtypeStruct((state_rows + payload, nobs), F32)] * gx_count,
        scratch_shapes=[
            pltpu.VMEM((gx_count, held, tile_rows, tile_cols), F32),
            pltpu.VMEM((payload, nobs), F32),
            pltpu.SMEM((batches,), jnp.int32),
            pltpu.VMEM((batches, nobs), jnp.int32),
            pltpu.VMEM((batches, nobs), F32),
            pltpu.SemaphoreType.DMA((gx_count,)),
            pltpu.SemaphoreType.DMA((gx_count,)),
            pltpu.SemaphoreType.DMA((3,)),
        ],
        name="pick",
    )(owner_device, obs_cells, weight, ensemble)
    for slot in range(1, gx_count):
        pieces[slot] = lax.ppermute(pieces[slot], "gx", [(i, i ^ slot) for i in range(gx_count)])
    state = lax.all_to_all(blocks, "gx", split_axis=0, concat_axis=0, tiled=True)
    *places, tapers = pl.pallas_call(
        functools.partial(tables_body, **geometry),
        in_specs=[in_smem, in_vmem],
        out_specs=[in_vmem] * 3,
        out_shape=[
            jax.ShapeDtypeStruct((batches, nobs, nobs), F32),
            jax.ShapeDtypeStruct((batches, nobs, tile_cols), F32),
            jax.ShapeDtypeStruct((len(pairs_of(batches)), nobs, nobs), F32),
        ],
        compiler_params=LIGHT,
        name="tables",
    )(owner_device, obs_cells)
    merge = pl.pallas_call(
        functools.partial(merge_body, base=state_rows, picks=picks),
        in_specs=[in_vmem] * gx_count,
        out_specs=in_vmem,
        out_shape=jax.ShapeDtypeStruct((gx_count * picks + pairs, nobs), F32),
        compiler_params=LIGHT,
        name="merge",
    )
    got = [merge(*pieces)]
    for step in range(1, gy_count):
        got.append(lax.ppermute(got[0], "gy", [(i, i ^ step) for i in range(gy_count)]))
    wide = -(-3 * members // nobs) * nobs
    chain = pl.pallas_call(
        functools.partial(chain_body, held=held, gx_count=gx_count, gy_count=gy_count),
        in_specs=[in_vmem] * (4 + gy_count),
        out_specs=[in_vmem] * 2,
        out_shape=[
            jax.ShapeDtypeStruct((batches, nobs, wide), BF16),
            jax.ShapeDtypeStruct((batches, 2 * members, 2 * nobs), BF16),
        ],
        scratch_shapes=[pltpu.VMEM((batches, members, nobs), F32)],
        compiler_params=LIGHT,
        name="chain",
    )
    factors = chain(obs_values, obs_error, weight, tapers, *got)
    tables = [*factors, *places]

    shape = (first, tile_rows, tile_cols)
    (upper,) = update(pieces, [], tables, 0, early, *shape, 1, inverse)
    upper = lax.all_to_all(
        upper.reshape(gx_count, held, early, tile_cols),
        "gx",
        split_axis=0,
        concat_axis=0,
        tiled=True,
    )
    state = state.reshape(members, rest, tile_cols)
    lower = [
        *update(
            pieces, [state], tables, early, tile_rows - early, *shape, gx_count, inverse
        )
    ]
    for slot in range(1, gx_count):
        lower[slot] = lax.ppermute(
            lower[slot], "gx", [(i, i ^ slot) for i in range(gx_count)]
        )
    return pl.pallas_call(
        functools.partial(assemble_body, first=early, tile_rows=tile_rows, here=ROWS),
        in_specs=[in_vmem] * (1 + gx_count),
        out_specs=in_hbm,
        out_shape=jax.ShapeDtypeStruct(ensemble.shape, F32),
        scratch_shapes=[pltpu.SemaphoreType.DMA((2 * gx_count,))],
        compiler_params=LIGHT,
        name="assemble",
    )(upper, *lower)


def solution(mesh):
    placed = (P("gx", None, "gy"), P(), P(), P(None, None, "gx", "gy"), P(), P())
    return jax.shard_map(
        local, mesh=mesh, in_specs=placed, out_specs=P("gx", None, "gy"), check_vma=False
    )
```

profile of v0, /device:TPU:0, one launch (start us, length us, event | category | flops | bytes accessed | tf_op | source)
XLA Modules:
  0.0 81.2 jit_solution(6195303350309851226)
XLA Ops:
  0.0 3.4 %pick.1 = (f32[8,2,32,256]{3,2,1,0:T(8,128)}, f32[144,128]{1,0:T(8,128)}, f32[144,128]{1,0:T(8,128)}, f32[144,128]{1,0:T(8,128)}, f32[144,128]{1,0:T(8,128)}, /*...) custom-call(s32[4]{0:T(128)} %owner_in.1, s32[4,128]{1,0:T(4,128)} %cells_in.1, ...), custom_call_target="tpu_custom_call" | custom-call | tf_op jit(solution)/shard_map/pick/pallas_call | solution.py:374
  3.5 7.4 %all-to-all-start.1 = ((f32[8,2,32,256]{3,2,1,0:T(8,128)}), f32[8,2,32,256]{3,2,1,0:T(8,128)S(1)}, u32[]{:S(2)}, u32[]{:S(2)}) async-start(f32[8,2,32,256]{3,2,1,0:T(8,128)} %get-tuple-element.40), calls=%async_computation.1 | async-start | bytes 1048576 | tf_op jit(solution)/shard_map/all_to_all | solution.py:396
  10.9 2.0 %collective-permute-start = (f32[144,128]{1,0:T(8,128)S(1)}, f32[144,128]{1,0:T(8,128)S(1)}, u32[]{:S(2)}, u32[]{:S(2)}) collective-permute-start(f32[144,128]{1,0:T(8,128)S(1)} %copy-done.12), channel_id=1, source_target_pairs={{0,4},{4,0},{8,12},{12,8},{16,20},{20,16},{24,28},{28,24},{1,5},{5... | collective-permute-start | bytes 221192 | tf_op jit(solution)/shard_map/ppermute | solution.py:395
  13.0 1.5 %collective-permute-start.1 = (f32[144,128]{1,0:T(8,128)S(1)}, f32[144,128]{1,0:T(8,128)S(1)}, u32[]{:S(2)}, u32[]{:S(2)}) collective-permute-start(f32[144,128]{1,0:T(8,128)S(1)} %copy-done.11), channel_id=1, source_target_pairs={{0,8},{4,12},{8,0},{12,4},{16,24},{20,28},{24,16},{28,20},{1,9},{5... | collective-permute-start | bytes 221192 | tf_op jit(solution)/shard_map/ppermute | solution.py:395
  14.5 2.8 %collective-permute-start.3 = (f32[144,128]{1,0:T(8,128)S(1)}, f32[144,128]{1,0:T(8,128)S(1)}, u32[]{:S(2)}, u32[]{:S(2)}) collective-permute-start(f32[144,128]{1,0:T(8,128)S(1)} %copy-done.9), channel_id=1, source_target_pairs={{0,16},{4,20},{8,24},{12,28},{16,0},{20,4},{24,8},{28,12},{1,17},{... | collective-permute-start | bytes 221192 | tf_op jit(solution)/shard_map/ppermute | solution.py:395
  17.4 1.5 %collective-permute-start.4 = (f32[144,128]{1,0:T(8,128)S(1)}, f32[144,128]{1,0:T(8,128)S(1)}, u32[]{:S(2)}, u32[]{:S(2)}) collective-permute-start(f32[144,128]{1,0:T(8,128)S(1)} %copy-done.8), channel_id=1, source_target_pairs={{0,20},{4,16},{8,28},{12,24},{16,4},{20,0},{24,12},{28,8},{1,21},{... | collective-permute-start | bytes 221192 | tf_op jit(solution)/shard_map/ppermute | solution.py:395
  18.8 3.7 %collective-permute-start.5 = (f32[144,128]{1,0:T(8,128)S(1)}, f32[144,128]{1,0:T(8,128)S(1)}, u32[]{:S(2)}, u32[]{:S(2)}) collective-permute-start(f32[144,128]{1,0:T(8,128)S(1)} %copy-done.7), channel_id=1, source_target_pairs={{0,24},{4,28},{8,16},{12,20},{16,8},{20,12},{24,0},{28,4},{1,25},{... | collective-permute-start | bytes 221192 | tf_op jit(solution)/shard_map/ppermute | solution.py:395
  22.6 4.5 %collective-permute-start.6 = (f32[144,128]{1,0:T(8,128)S(1)}, f32[144,128]{1,0:T(8,128)S(1)}, u32[]{:S(2)}, u32[]{:S(2)}) collective-permute-start(f32[144,128]{1,0:T(8,128)S(1)} %copy-done.6), channel_id=1, source_target_pairs={{0,28},{4,24},{8,20},{12,16},{16,12},{20,8},{24,4},{28,0},{1,29},{... | collective-permute-start | bytes 221192 | tf_op jit(solution)/shard_map/ppermute | solution.py:395
  27.1 7.7 %collective-permute-done.3.refs_4_ = f32[144,128]{1,0:T(8,128)S(1)} collective-permute-done((f32[144,128]{1,0:T(8,128)S(1)}, f32[144,128]{1,0:T(8,128)S(1)}, u32[]{:S(2)}, u32[]{:S(2)}) %collective-permute-start.3) | collective-permute-done | bytes 73760 | tf_op jit(solution)/shard_map/ppermute | solution.py:395
  34.7 2.1 %collective-permute-done.4.refs_5_ = f32[144,128]{1,0:T(8,128)S(1)} collective-permute-done((f32[144,128]{1,0:T(8,128)S(1)}, f32[144,128]{1,0:T(8,128)S(1)}, u32[]{:S(2)}, u32[]{:S(2)}) %collective-permute-start.4) | collective-permute-done | bytes 73760 | tf_op jit(solution)/shard_map/ppermute | solution.py:395
  37.0 1.6 %collective-permute-start.8 = (f32[72,128]{1,0:T(8,128)S(1)}, f32[72,128]{1,0:T(8,128)S(1)}, u32[]{:S(2)}, u32[]{:S(2)}) collective-permute-start(f32[72,128]{1,0:T(8,128)S(1)} %merge.1.refs_0_), channel_id=1, source_target_pairs={{0,2},{1,3},{2,0},{3,1},{4,6},{5,7},{6,4},{7,5},{8,10},{9,11},{10,... | collective-permute-start | bytes 110600 | tf_op jit(solution)/shard_map/ppermute | solution.py:419
  38.8 0.8 tables.1
  39.6 1.1 %collective-permute-done.9.refs_3_ = f32[72,128]{1,0:T(8,128)S(1)} collective-permute-done((f32[72,128]{1,0:T(8,128)S(1)}, f32[72,128]{1,0:T(8,128)S(1)}, u32[]{:S(2)}, u32[]{:S(2)}) %collective-permute-start.9) | collective-permute-done | bytes 36896 | tf_op jit(solution)/shard_map/ppermute | solution.py:419
  41.2 1.3 %chain.1 = (bf16[4,128,128]{2,1,0:T(8,128)(2,1)S(1)}, bf16[4,32,256]{2,1,0:T(8,128)(2,1)S(1)}) custom-call(f32[4,128]{1,0:T(4,128)S(1)} %copy-done.3, f32[4,128]{1,0:T(4,128)S(1)} %copy-done.4, f32[4,128]{1,0:T(4,128)S(1)} %bitcast.5, f32[6,128,128]{2,1,0:T(8,128)S(1)} %get-tuple-element.27.taper_ref, f32[72,128]{1,0:T(8,128)S(1)} %merge.1.refs_0_, ...), custom_call_target="tpu_custom_call" | custom-call | tf_op jit(solution)/shard_map/chain/pallas_call | solution.py:433
  42.4 4.9 %update.2 = f32[16,24,256]{2,1,0:T(8,128)} custom-call(bf16[4,128,128]{2,1,0:T(8,128)(2,1)S(1)} %get-tuple-element.36.a_ref, bf16[4,32,256]{2,1,0:T(8,128)(2,1)S(1)} %get-tuple-element.37.w_ref, f32[4,128,128]{2,1,0:T(8,128)S(1)} %get-tuple-element.38.x_ref, f32[4,128,256]{2,1,0:T(8,128)S(1)} %get-tuple-element.39.y_ref, f32[144,128]{1,0:T(8,128)S(1)} %copy-done, ...), custom_call_target="tpu_custom_call" | custom-call | flops 503316480 | bytes 786432 | tf_op jit(solution)/shard_map/update/pallas_call | solution.py:300
  47.3 4.9 %all-to-all-start = ((f32[8,2,24,256]{3,2,1,0:T(8,128)}), f32[8,2,24,256]{3,2,1,0:T(8,128)S(1)}, u32[]{:S(2)}, u32[]{:S(2)}) async-start(f32[8,2,24,256]{3,2,1,0:T(8,128)} %bitcast.1), calls=%async_computation | async-start | bytes 786432 | tf_op jit(solution)/shard_map/all_to_all | solution.py:438
  52.2 8.2 %update.3 = (f32[2,40,256]{2,1,0:T(8,128)S(1)}, f32[2,40,256]{2,1,0:T(8,128)S(1)}, f32[2,40,256]{2,1,0:T(8,128)S(1)}, f32[2,40,256]{2,1,0:T(8,128)S(1)}, f32[2,4...) custom-call(bf16[4,128,128]{2,1,0:T(8,128)(2,1)S(1)} %get-tuple-element.3, ...), custom_call_target="tpu_custom_call" | custom-call | flops 838860800 | bytes 1310720 | tf_op jit(solution)/shard_map/update/pallas_call | solution.py:300
  60.5 2.1 %collective-permute-start.10 = (f32[2,40,256]{2,1,0:T(8,128)S(1)}, f32[2,40,256]{2,1,0:T(8,128)S(1)}, u32[]{:S(2)}, u32[]{:S(2)}) collective-permute-start(f32[2,40,256]{2,1,0:T(8,128)S(1)} %get-tuple-element.42), channel_id=1, source_target_pairs={{0,4},{4,0},{8,12},{12,8},{16,20},{20,16},{24,28},{28,24},{1,5},{5... | collective-permute-start | bytes 245768 | tf_op jit(solution)/shard_map/ppermute | solution.py:452
  62.6 1.5 %collective-permute-start.11 = (f32[2,40,256]{2,1,0:T(8,128)S(1)}, f32[2,40,256]{2,1,0:T(8,128)S(1)}, u32[]{:S(2)}, u32[]{:S(2)}) collective-permute-start(f32[2,40,256]{2,1,0:T(8,128)S(1)} %get-tuple-element.43), channel_id=1, source_target_pairs={{0,8},{4,12},{8,0},{12,4},{16,24},{20,28},{24,16},{28,20},{1,9},{5... | collective-permute-start | bytes 245768 | tf_op jit(solution)/shard_map/ppermute | solution.py:452
  64.1 2.9 %collective-permute-start.13 = (f32[2,40,256]{2,1,0:T(8,128)S(1)}, f32[2,40,256]{2,1,0:T(8,128)S(1)}, u32[]{:S(2)}, u32[]{:S(2)}) collective-permute-start(f32[2,40,256]{2,1,0:T(8,128)S(1)} %get-tuple-element.45), channel_id=1, source_target_pairs={{0,16},{4,20},{8,24},{12,28},{16,0},{20,4},{24,8},{28,12},{1,17},{... | collective-permute-start | bytes 245768 | tf_op jit(solution)/shard_map/ppermute | solution.py:452
  67.0 1.5 %collective-permute-start.14 = (f32[2,40,256]{2,1,0:T(8,128)S(1)}, f32[2,40,256]{2,1,0:T(8,128)S(1)}, u32[]{:S(2)}, u32[]{:S(2)}) collective-permute-start(f32[2,40,256]{2,1,0:T(8,128)S(1)} %get-tuple-element.46), channel_id=1, source_target_pairs={{0,20},{4,16},{8,28},{12,24},{16,4},{20,0},{24,12},{28,8},{1,21},{... | collective-permute-start | bytes 245768 | tf_op jit(solution)/shard_map/ppermute | solution.py:452
  68.4 3.3 %collective-permute-start.15 = (f32[2,40,256]{2,1,0:T(8,128)S(1)}, f32[2,40,256]{2,1,0:T(8,128)S(1)}, u32[]{:S(2)}, u32[]{:S(2)}) collective-permute-start(f32[2,40,256]{2,1,0:T(8,128)S(1)} %get-tuple-element.47), channel_id=1, source_target_pairs={{0,24},{4,28},{8,16},{12,20},{16,8},{20,12},{24,0},{28,4},{1,25},{... | collective-permute-start | bytes 245768 | tf_op jit(solution)/shard_map/ppermute | solution.py:452
  71.8 8.3 %collective-permute-done.14.refs_5_ = f32[2,40,256]{2,1,0:T(8,128)S(1)} collective-permute-done((f32[2,40,256]{2,1,0:T(8,128)S(1)}, f32[2,40,256]{2,1,0:T(8,128)S(1)}, u32[]{:S(2)}, u32[]{:S(2)}) %collective-permute-start.14) | collective-permute-done | bytes 81952 | tf_op jit(solution)/shard_map/ppermute | solution.py:452
  80.1 1.1 %assemble.1 = f32[2,512,256]{2,1,0:T(8,128)} custom-call(f32[8,2,24,256]{3,2,1,0:T(8,128)S(1)} %all-to-all-done.whole_ref, f32[2,40,256]{2,1,0:T(8,128)S(1)} %get-tuple-element.41.refs_0_, f32[2,40,256]{2,1,0:T(8,128)S(1)} %collective-permute-done.10.refs_1_, f32[2,40,256]{2,1,0:T(8,128)S(1)} %collective-permute-done.11.refs_2_, ...), custom_call_target="tpu_custom_call" | custom-call | tf_op jit(solution)/shard_map/assemble/pallas_call | solution.py:455
  (47 shorter events, 1.1 us)
Async XLA Ops:
  3.5 11.1 %copy-start.9 = (f32[144,128]{1,0:T(8,128)S(1)}, f32[144,128]{1,0:T(8,128)}, u32[]{:S(2)}) copy-start(f32[144,128]{1,0:T(8,128)} %get-tuple-element.32) | copy-start | bytes 221188
  3.5 13.9 %copy-start.8 = (f32[144,128]{1,0:T(8,128)S(1)}, f32[144,128]{1,0:T(8,128)}, u32[]{:S(2)}) copy-start(f32[144,128]{1,0:T(8,128)} %get-tuple-element.33) | copy-start | bytes 221188
  3.5 15.3 %copy-start.7 = (f32[144,128]{1,0:T(8,128)S(1)}, f32[144,128]{1,0:T(8,128)}, u32[]{:S(2)}) copy-start(f32[144,128]{1,0:T(8,128)} %get-tuple-element.34) | copy-start | bytes 221188
  3.5 19.1 %copy-start.6 = (f32[144,128]{1,0:T(8,128)S(1)}, f32[144,128]{1,0:T(8,128)}, u32[]{:S(2)}) copy-start(f32[144,128]{1,0:T(8,128)} %get-tuple-element.35) | copy-start | bytes 221188
  3.5 33.3 %copy-start = (f32[144,128]{1,0:T(8,128)S(1)}, f32[144,128]{1,0:T(8,128)}, u32[]{:S(2)}) copy-start(f32[144,128]{1,0:T(8,128)} %get-tuple-element.28.refs_0_) | copy-start | bytes 221188
  3.5 43.8 %all-to-all-start.1 = ((f32[8,2,32,256]{3,2,1,0:T(8,128)}), f32[8,2,32,256]{3,2,1,0:T(8,128)S(1)}, u32[]{:S(2)}, u32[]{:S(2)}) async-start(f32[8,2,32,256]{3,2,1,0:T(8,128)} %get-tuple-element.40), calls=%async_computation.1 | async-start | bytes 1048576 | tf_op jit(solution)/shard_map/all_to_all | solution.py:396
  10.9 7.9 %collective-permute-start = (f32[144,128]{1,0:T(8,128)S(1)}, f32[144,128]{1,0:T(8,128)S(1)}, u32[]{:S(2)}, u32[]{:S(2)}) collective-permute-start(f32[144,128]{1,0:T(8,128)S(1)} %copy-done.12), channel_id=1, source_target_pairs={{0,4},{4,0},{8,12},{12,8},{16,20},{20,16},{24,28},{28,24},{1,5},{5... | collective-permute-start | bytes 221192 | tf_op jit(solution)/shard_map/ppermute | solution.py:395
  13.0 9.6 %collective-permute-start.1 = (f32[144,128]{1,0:T(8,128)S(1)}, f32[144,128]{1,0:T(8,128)S(1)}, u32[]{:S(2)}, u32[]{:S(2)}) collective-permute-start(f32[144,128]{1,0:T(8,128)S(1)} %copy-done.11), channel_id=1, source_target_pairs={{0,8},{4,12},{8,0},{12,4},{16,24},{20,28},{24,16},{28,20},{1,9},{5... | collective-permute-start | bytes 221192 | tf_op jit(solution)/shard_map/ppermute | solution.py:395
  14.4 12.6 %collective-permute-start.2 = (f32[144,128]{1,0:T(8,128)S(1)}, f32[144,128]{1,0:T(8,128)S(1)}, u32[]{:S(2)}, u32[]{:S(2)}) collective-permute-start(f32[144,128]{1,0:T(8,128)S(1)} %copy-done.10), channel_id=1, source_target_pairs={{0,12},{4,8},{8,4},{12,0},{16,28},{20,24},{24,20},{28,16},{1,13},{... | collective-permute-start | bytes 221192 | tf_op jit(solution)/shard_map/ppermute | solution.py:395
  14.5 20.2 %collective-permute-start.3 = (f32[144,128]{1,0:T(8,128)S(1)}, f32[144,128]{1,0:T(8,128)S(1)}, u32[]{:S(2)}, u32[]{:S(2)}) collective-permute-start(f32[144,128]{1,0:T(8,128)S(1)} %copy-done.9), channel_id=1, source_target_pairs={{0,16},{4,20},{8,24},{12,28},{16,0},{20,4},{24,8},{28,12},{1,17},{... | collective-permute-start | bytes 221192 | tf_op jit(solution)/shard_map/ppermute | solution.py:395
  17.4 19.4 %collective-permute-start.4 = (f32[144,128]{1,0:T(8,128)S(1)}, f32[144,128]{1,0:T(8,128)S(1)}, u32[]{:S(2)}, u32[]{:S(2)}) collective-permute-start(f32[144,128]{1,0:T(8,128)S(1)} %copy-done.8), channel_id=1, source_target_pairs={{0,20},{4,16},{8,28},{12,24},{16,4},{20,0},{24,12},{28,8},{1,21},{... | collective-permute-start | bytes 221192 | tf_op jit(solution)/shard_map/ppermute | solution.py:395
  18.8 18.0 %collective-permute-start.5 = (f32[144,128]{1,0:T(8,128)S(1)}, f32[144,128]{1,0:T(8,128)S(1)}, u32[]{:S(2)}, u32[]{:S(2)}) collective-permute-start(f32[144,128]{1,0:T(8,128)S(1)} %copy-done.7), channel_id=1, source_target_pairs={{0,24},{4,28},{8,16},{12,20},{16,8},{20,12},{24,0},{28,4},{1,25},{... | collective-permute-start | bytes 221192 | tf_op jit(solution)/shard_map/ppermute | solution.py:395
  22.6 14.2 %collective-permute-start.6 = (f32[144,128]{1,0:T(8,128)S(1)}, f32[144,128]{1,0:T(8,128)S(1)}, u32[]{:S(2)}, u32[]{:S(2)}) collective-permute-start(f32[144,128]{1,0:T(8,128)S(1)} %copy-done.6), channel_id=1, source_target_pairs={{0,28},{4,24},{8,20},{12,16},{16,12},{20,8},{24,4},{28,0},{1,29},{... | collective-permute-start | bytes 221192 | tf_op jit(solution)/shard_map/ppermute | solution.py:395
  36.9 3.8 %collective-permute-start.9 = (f32[72,128]{1,0:T(8,128)S(1)}, f32[72,128]{1,0:T(8,128)S(1)}, u32[]{:S(2)}, u32[]{:S(2)}) collective-permute-start(f32[72,128]{1,0:T(8,128)S(1)} %merge.1.refs_0_), channel_id=1, source_target_pairs={{0,3},{1,2},{2,1},{3,0},{4,7},{5,6},{6,5},{7,4},{8,11},{9,10},{10,... | collective-permute-start | bytes 110600 | tf_op jit(solution)/shard_map/ppermute | solution.py:419
  37.0 4.2 %collective-permute-start.8 = (f32[72,128]{1,0:T(8,128)S(1)}, f32[72,128]{1,0:T(8,128)S(1)}, u32[]{:S(2)}, u32[]{:S(2)}) collective-permute-start(f32[72,128]{1,0:T(8,128)S(1)} %merge.1.refs_0_), channel_id=1, source_target_pairs={{0,2},{1,3},{2,0},{3,1},{4,6},{5,7},{6,4},{7,5},{8,10},{9,11},{10,... | collective-permute-start | bytes 110600 | tf_op jit(solution)/shard_map/ppermute | solution.py:419
  38.6 2.6 %collective-permute-start.7 = (f32[72,128]{1,0:T(8,128)S(1)}, f32[72,128]{1,0:T(8,128)S(1)}, u32[]{:S(2)}, u32[]{:S(2)}) collective-permute-start(f32[72,128]{1,0:T(8,128)S(1)} %merge.1.refs_0_), channel_id=1, source_target_pairs={{0,1},{1,0},{2,3},{3,2},{4,5},{5,4},{6,7},{7,6},{8,9},{9,8},{10,11... | collective-permute-start | bytes 110600 | tf_op jit(solution)/shard_map/ppermute | solution.py:419
  47.3 24.5 %all-to-all-start = ((f32[8,2,24,256]{3,2,1,0:T(8,128)}), f32[8,2,24,256]{3,2,1,0:T(8,128)S(1)}, u32[]{:S(2)}, u32[]{:S(2)}) async-start(f32[8,2,24,256]{3,2,1,0:T(8,128)} %bitcast.1), calls=%async_computation | async-start | bytes 786432 | tf_op jit(solution)/shard_map/all_to_all | solution.py:438
  60.5 7.9 %collective-permute-start.10 = (f32[2,40,256]{2,1,0:T(8,128)S(1)}, f32[2,40,256]{2,1,0:T(8,128)S(1)}, u32[]{:S(2)}, u32[]{:S(2)}) collective-permute-start(f32[2,40,256]{2,1,0:T(8,128)S(1)} %get-tuple-element.42), channel_id=1, source_target_pairs={{0,4},{4,0},{8,12},{12,8},{16,20},{20,16},{24,28},{28,24},{1,5},{5... | collective-permute-start | bytes 245768 | tf_op jit(solution)/shard_map/ppermute | solution.py:452
  62.6 9.1 %collective-permute-start.11 = (f32[2,40,256]{2,1,0:T(8,128)S(1)}, f32[2,40,256]{2,1,0:T(8,128)S(1)}, u32[]{:S(2)}, u32[]{:S(2)}) collective-permute-start(f32[2,40,256]{2,1,0:T(8,128)S(1)} %get-tuple-element.43), channel_id=1, source_target_pairs={{0,8},{4,12},{8,0},{12,4},{16,24},{20,28},{24,16},{28,20},{1,9},{5... | collective-permute-start | bytes 245768 | tf_op jit(solution)/shard_map/ppermute | solution.py:452
  64.0 7.7 %collective-permute-start.12 = (f32[2,40,256]{2,1,0:T(8,128)S(1)}, f32[2,40,256]{2,1,0:T(8,128)S(1)}, u32[]{:S(2)}, u32[]{:S(2)}) collective-permute-start(f32[2,40,256]{2,1,0:T(8,128)S(1)} %get-tuple-element.44), channel_id=1, source_target_pairs={{0,12},{4,8},{8,4},{12,0},{16,28},{20,24},{24,20},{28,16},{1,13},{... | collective-permute-start | bytes 245768 | tf_op jit(solution)/shard_map/ppermute | solution.py:452
  64.1 7.7 %collective-permute-start.13 = (f32[2,40,256]{2,1,0:T(8,128)S(1)}, f32[2,40,256]{2,1,0:T(8,128)S(1)}, u32[]{:S(2)}, u32[]{:S(2)}) collective-permute-start(f32[2,40,256]{2,1,0:T(8,128)S(1)} %get-tuple-element.45), channel_id=1, source_target_pairs={{0,16},{4,20},{8,24},{12,28},{16,0},{20,4},{24,8},{28,12},{1,17},{... | collective-permute-start | bytes 245768 | tf_op jit(solution)/shard_map/ppermute | solution.py:452
  67.0 13.1 %collective-permute-start.14 = (f32[2,40,256]{2,1,0:T(8,128)S(1)}, f32[2,40,256]{2,1,0:T(8,128)S(1)}, u32[]{:S(2)}, u32[]{:S(2)}) collective-permute-start(f32[2,40,256]{2,1,0:T(8,128)S(1)} %get-tuple-element.46), channel_id=1, source_target_pairs={{0,20},{4,16},{8,28},{12,24},{16,4},{20,0},{24,12},{28,8},{1,21},{... | collective-permute-start | bytes 245768 | tf_op jit(solution)/shard_map/ppermute | solution.py:452
  68.4 11.7 %collective-permute-start.15 = (f32[2,40,256]{2,1,0:T(8,128)S(1)}, f32[2,40,256]{2,1,0:T(8,128)S(1)}, u32[]{:S(2)}, u32[]{:S(2)}) collective-permute-start(f32[2,40,256]{2,1,0:T(8,128)S(1)} %get-tuple-element.47), channel_id=1, source_target_pairs={{0,24},{4,28},{8,16},{12,20},{16,8},{20,12},{24,0},{28,4},{1,25},{... | collective-permute-start | bytes 245768 | tf_op jit(solution)/shard_map/ppermute | solution.py:452
  71.7 8.4 %collective-permute-start.16 = (f32[2,40,256]{2,1,0:T(8,128)S(1)}, f32[2,40,256]{2,1,0:T(8,128)S(1)}, u32[]{:S(2)}, u32[]{:S(2)}) collective-permute-start(f32[2,40,256]{2,1,0:T(8,128)S(1)} %get-tuple-element.48), channel_id=1, source_target_pairs={{0,28},{4,24},{8,20},{12,16},{16,12},{20,8},{24,4},{28,0},{1,29},{... | collective-permute-start | bytes 245768 | tf_op jit(solution)/shard_map/ppermute | solution.py:452
  (8 other events, 44.9 us)
where the time goes:
time: 81.6 us; the launch traced here: 81.2 us
  starting transfers between devices  41.6 us (51%)
  Pallas kernels  19.7 us (24%)
  waiting for transfers between devices  19.6 us (24%)
    ppermute x7, starting transfers between devices, local(): lax.ppermute(pieces[slot], 'gx', [(i, i ^ slot) for i in range(gx_count)])  16.1 us
    pallas_call x2, Pallas kernels, update(): pl.pallas_call(functools.partial(update_body, first=first, depth=depth, t...  13.1 us
    ppermute x7, starting transfers between devices, local(): lax.ppermute(lower[slot], 'gx', [(i, i ^ slot) for i in range(gx_count)])  11.3 us
    ppermute x7, waiting for transfers between devices, local(): lax.ppermute(pieces[slot], 'gx', [(i, i ^ slot) for i in range(gx_count)])  9.77 us
    ppermute x7, waiting for transfers between devices, local(): lax.ppermute(lower[slot], 'gx', [(i, i ^ slot) for i in range(gx_count)])  8.32 us
    all_to_all x1, starting transfers between devices, local(): lax.all_to_all(blocks, 'gx', split_axis=0, concat_axis=0, tiled=True)  7.43 us
    all_to_all x1, starting transfers between devices, local(): lax.all_to_all(upper.reshape(gx_count, held, early, tile_cols), 'gx', spl...  4.9 us
    pallas_call x1, Pallas kernels, local(): pl.pallas_call(functools.partial(pick_body, tile_rows=tile_rows, first=fi...  3.42 us
  transfers between devices with their start and end apart: 19, of which 5 were waited for; matrix products, arithmetic and copies ran while one was open for 0% of the time, Pallas kernels for 19%

commit v1 on v0

--- a/solution.py
+++ b/solution.py
@@ -12,6 +12,7 @@
 IN_EIGHTHS = 4
 OUT_EIGHTHS = 3
 LIGHT = pltpu.CompilerParams(vmem_limit_bytes=16 << 20)
+SPREAD = pltpu.CompilerParams(vmem_limit_bytes=16 << 20)
 ROWS = 8
 F32 = jnp.float32
 BF16 = jnp.bfloat16
@@ -85,7 +86,6 @@
         hits.append((jnp.concatenate([row_hit] * 3, axis=0), col_hit))
     for tile in range(gx_count):
         fetch(tile).wait()
-    for tile in range(gx_count):
         put(tile).start()
     folds = cols // nobs
     for slot in range(gx_count):
@@ -149,6 +149,12 @@
         taper_ref[at] = pl.reciprocal(1.0 + (dx * dx + dy * dy))
 
 
+def once(array):
+    return pl.BlockSpec(
+        array.shape, lambda i: (0,) * array.ndim, pipeline_mode=pl.Buffered(1)
+    )
+
+
 def merge_body(*refs, base, picks):
     pieces, out_ref = refs[:-1], refs[-1]
     total = None
@@ -286,10 +292,6 @@
             target[...] = to_ref[pl.ds(held * (row_at ^ slot), held)]
 
 
-def whole(array):
-    return pl.BlockSpec(array.shape, lambda i: (0,) * array.ndim)
-
-
 def update(pieces, others, tables, first, count, depth, tile_rows, cols, outs, inverse):
     gx_count = len(pieces)
     batches, nobs, _ = tables[2].shape
@@ -307,7 +309,7 @@
             inverse=inverse,
         ),
         grid=(count // rows,),
-        in_specs=[whole(array) for array in (*tables, *pieces)]
+        in_specs=[once(array) for array in (*tables, *pieces)]
         + [
             pl.BlockSpec(
                 (members, rows, cols),
@@ -323,7 +325,7 @@
             bytes_accessed=8 * members * count * cols,
             transcendentals=cells,
         ),
-        compiler_params=LIGHT,
+        compiler_params=LIGHT if others else SPREAD,
         name="update",
     )(*tables, *pieces, *others)
 

time: 81.6 us -> 81.2 us (level)
  no operation moved by 1% of the time
where the time goes in v1:
time: 81.2 us; the launch traced here: 80.9 us
  starting transfers between devices  41.6 us (51%)
  waiting for transfers between devices  19.7 us (24%)
  Pallas kernels  19.3 us (24%)
    ppermute x7, starting transfers between devices, local(): lax.ppermute(pieces[slot], 'gx', [(i, i ^ slot) for i in range(gx_count)])  16.1 us
    pallas_call x2, Pallas kernels, update(): pl.pallas_call(functools.partial(update_body, first=first, depth=depth, t...  13.1 us
    ppermute x7, starting transfers between devices, local(): lax.ppermute(lower[slot], 'gx', [(i, i ^ slot) for i in range(gx_count)])  11.3 us
    ppermute x7, waiting for transfers between devices, local(): lax.ppermute(pieces[slot], 'gx', [(i, i ^ slot) for i in range(gx_count)])  9.77 us
    ppermute x7, waiting for transfers between devices, local(): lax.ppermute(lower[slot], 'gx', [(i, i ^ slot) for i in range(gx_count)])  8.33 us
    all_to_all x1, starting transfers between devices, local(): lax.all_to_all(blocks, 'gx', split_axis=0, concat_axis=0, tiled=True)  7.43 us
    all_to_all x1, starting transfers between devices, local(): lax.all_to_all(upper.reshape(gx_count, held, early, tile_cols), 'gx', spl...  4.89 us
    pallas_call x1, Pallas kernels, local(): pl.pallas_call(functools.partial(pick_body, tile_rows=tile_rows, first=fi...  3.07 us
  transfers between devices with their start and end apart: 19, of which 5 were waited for; matrix products, arithmetic and copies ran while one was open for 0% of the time, Pallas kernels for 19%

profile of v1, /device:TPU:0, one launch (start us, length us, event | category | flops | bytes accessed | tf_op | source)
XLA Modules:
  0.0 80.9 jit_solution(15630125636713496227)
XLA Ops:
  0.0 3.1 %pick.1 = (f32[8,2,32,256]{3,2,1,0:T(8,128)}, f32[144,128]{1,0:T(8,128)}, f32[144,128]{1,0:T(8,128)}, f32[144,128]{1,0:T(8,128)}, f32[144,128]{1,0:T(8,128)}, /*...) custom-call(s32[4]{0:T(128)} %owner_in.1, s32[4,128]{1,0:T(4,128)} %cells_in.1, ...), custom_call_target="tpu_custom_call" | custom-call | tf_op jit(solution)/shard_map/pick/pallas_call | solution.py:376
  3.2 7.4 %all-to-all-start.1 = ((f32[8,2,32,256]{3,2,1,0:T(8,128)}), f32[8,2,32,256]{3,2,1,0:T(8,128)S(1)}, u32[]{:S(2)}, u32[]{:S(2)}) async-start(f32[8,2,32,256]{3,2,1,0:T(8,128)} %get-tuple-element.40), calls=%async_computation.1 | async-start | bytes 1048576 | tf_op jit(solution)/shard_map/all_to_all | solution.py:398
  10.6 2.0 %collective-permute-start = (f32[144,128]{1,0:T(8,128)S(1)}, f32[144,128]{1,0:T(8,128)S(1)}, u32[]{:S(2)}, u32[]{:S(2)}) collective-permute-start(f32[144,128]{1,0:T(8,128)S(1)} %copy-done.12), channel_id=1, source_target_pairs={{0,4},{4,0},{8,12},{12,8},{16,20},{20,16},{24,28},{28,24},{1,5},{5... | collective-permute-start | bytes 221192 | tf_op jit(solution)/shard_map/ppermute | solution.py:397
  12.6 1.5 %collective-permute-start.1 = (f32[144,128]{1,0:T(8,128)S(1)}, f32[144,128]{1,0:T(8,128)S(1)}, u32[]{:S(2)}, u32[]{:S(2)}) collective-permute-start(f32[144,128]{1,0:T(8,128)S(1)} %copy-done.11), channel_id=1, source_target_pairs={{0,8},{4,12},{8,0},{12,4},{16,24},{20,28},{24,16},{28,20},{1,9},{5... | collective-permute-start | bytes 221192 | tf_op jit(solution)/shard_map/ppermute | solution.py:397
  14.2 2.8 %collective-permute-start.3 = (f32[144,128]{1,0:T(8,128)S(1)}, f32[144,128]{1,0:T(8,128)S(1)}, u32[]{:S(2)}, u32[]{:S(2)}) collective-permute-start(f32[144,128]{1,0:T(8,128)S(1)} %copy-done.9), channel_id=1, source_target_pairs={{0,16},{4,20},{8,24},{12,28},{16,0},{20,4},{24,8},{28,12},{1,17},{... | collective-permute-start | bytes 221192 | tf_op jit(solution)/shard_map/ppermute | solution.py:397
  17.0 1.5 %collective-permute-start.4 = (f32[144,128]{1,0:T(8,128)S(1)}, f32[144,128]{1,0:T(8,128)S(1)}, u32[]{:S(2)}, u32[]{:S(2)}) collective-permute-start(f32[144,128]{1,0:T(8,128)S(1)} %copy-done.8), channel_id=1, source_target_pairs={{0,20},{4,16},{8,28},{12,24},{16,4},{20,0},{24,12},{28,8},{1,21},{... | collective-permute-start | bytes 221192 | tf_op jit(solution)/shard_map/ppermute | solution.py:397
  18.5 3.7 %collective-permute-start.5 = (f32[144,128]{1,0:T(8,128)S(1)}, f32[144,128]{1,0:T(8,128)S(1)}, u32[]{:S(2)}, u32[]{:S(2)}) collective-permute-start(f32[144,128]{1,0:T(8,128)S(1)} %copy-done.7), channel_id=1, source_target_pairs={{0,24},{4,28},{8,16},{12,20},{16,8},{20,12},{24,0},{28,4},{1,25},{... | collective-permute-start | bytes 221192 | tf_op jit(solution)/shard_map/ppermute | solution.py:397
  22.2 4.5 %collective-permute-start.6 = (f32[144,128]{1,0:T(8,128)S(1)}, f32[144,128]{1,0:T(8,128)S(1)}, u32[]{:S(2)}, u32[]{:S(2)}) collective-permute-start(f32[144,128]{1,0:T(8,128)S(1)} %copy-done.6), channel_id=1, source_target_pairs={{0,28},{4,24},{8,20},{12,16},{16,12},{20,8},{24,4},{28,0},{1,29},{... | collective-permute-start | bytes 221192 | tf_op jit(solution)/shard_map/ppermute | solution.py:397
  26.7 7.7 %collective-permute-done.3.refs_4_ = f32[144,128]{1,0:T(8,128)S(1)} collective-permute-done((f32[144,128]{1,0:T(8,128)S(1)}, f32[144,128]{1,0:T(8,128)S(1)}, u32[]{:S(2)}, u32[]{:S(2)}) %collective-permute-start.3) | collective-permute-done | bytes 73760 | tf_op jit(solution)/shard_map/ppermute | solution.py:397
  34.4 2.1 %collective-permute-done.4.refs_5_ = f32[144,128]{1,0:T(8,128)S(1)} collective-permute-done((f32[144,128]{1,0:T(8,128)S(1)}, f32[144,128]{1,0:T(8,128)S(1)}, u32[]{:S(2)}, u32[]{:S(2)}) %collective-permute-start.4) | collective-permute-done | bytes 73760 | tf_op jit(solution)/shard_map/ppermute | solution.py:397
  36.6 1.6 %collective-permute-start.8 = (f32[72,128]{1,0:T(8,128)S(1)}, f32[72,128]{1,0:T(8,128)S(1)}, u32[]{:S(2)}, u32[]{:S(2)}) collective-permute-start(f32[72,128]{1,0:T(8,128)S(1)} %merge.1.refs_0_), channel_id=1, source_target_pairs={{0,2},{1,3},{2,0},{3,1},{4,6},{5,7},{6,4},{7,5},{8,10},{9,11},{10,... | collective-permute-start | bytes 110600 | tf_op jit(solution)/shard_map/ppermute | solution.py:421
  38.5 0.8 tables.1
  39.2 1.1 %collective-permute-done.9.refs_3_ = f32[72,128]{1,0:T(8,128)S(1)} collective-permute-done((f32[72,128]{1,0:T(8,128)S(1)}, f32[72,128]{1,0:T(8,128)S(1)}, u32[]{:S(2)}, u32[]{:S(2)}) %collective-permute-start.9) | collective-permute-done | bytes 36896 | tf_op jit(solution)/shard_map/ppermute | solution.py:421
  40.8 1.3 %chain.1 = (bf16[4,128,128]{2,1,0:T(8,128)(2,1)S(1)}, bf16[4,32,256]{2,1,0:T(8,128)(2,1)S(1)}) custom-call(f32[4,128]{1,0:T(4,128)S(1)} %copy-done.3, f32[4,128]{1,0:T(4,128)S(1)} %copy-done.4, f32[4,128]{1,0:T(4,128)S(1)} %bitcast.5, f32[6,128,128]{2,1,0:T(8,128)S(1)} %get-tuple-element.27.taper_ref, f32[72,128]{1,0:T(8,128)S(1)} %merge.1.refs_0_, ...), custom_call_target="tpu_custom_call" | custom-call | tf_op jit(solution)/shard_map/chain/pallas_call | solution.py:435
  42.1 4.9 %update.2 = f32[16,24,256]{2,1,0:T(8,128)} custom-call(bf16[4,128,128]{2,1,0:T(8,128)(2,1)S(1)} %get-tuple-element.36.a_ref, bf16[4,32,256]{2,1,0:T(8,128)(2,1)S(1)} %get-tuple-element.37.w_ref, f32[4,128,128]{2,1,0:T(8,128)S(1)} %get-tuple-element.38.x_ref, f32[4,128,256]{2,1,0:T(8,128)S(1)} %get-tuple-element.39.y_ref, f32[144,128]{1,0:T(8,128)S(1)} %copy-done, ...), custom_call_target="tpu_custom_call" | custom-call | flops 503316480 | bytes 786432 | tf_op jit(solution)/shard_map/update/pallas_call | solution.py:302
  47.0 4.9 %all-to-all-start = ((f32[8,2,24,256]{3,2,1,0:T(8,128)}), f32[8,2,24,256]{3,2,1,0:T(8,128)S(1)}, u32[]{:S(2)}, u32[]{:S(2)}) async-start(f32[8,2,24,256]{3,2,1,0:T(8,128)} %bitcast.1), calls=%async_computation | async-start | bytes 786432 | tf_op jit(solution)/shard_map/all_to_all | solution.py:440
  51.9 8.2 %update.3 = (f32[2,40,256]{2,1,0:T(8,128)S(1)}, f32[2,40,256]{2,1,0:T(8,128)S(1)}, f32[2,40,256]{2,1,0:T(8,128)S(1)}, f32[2,40,256]{2,1,0:T(8,128)S(1)}, f32[2,4...) custom-call(bf16[4,128,128]{2,1,0:T(8,128)(2,1)S(1)} %get-tuple-element.3, ...), custom_call_target="tpu_custom_call" | custom-call | flops 838860800 | bytes 1310720 | tf_op jit(solution)/shard_map/update/pallas_call | solution.py:302
  60.1 2.1 %collective-permute-start.10 = (f32[2,40,256]{2,1,0:T(8,128)S(1)}, f32[2,40,256]{2,1,0:T(8,128)S(1)}, u32[]{:S(2)}, u32[]{:S(2)}) collective-permute-start(f32[2,40,256]{2,1,0:T(8,128)S(1)} %get-tuple-element.42), channel_id=1, source_target_pairs={{0,4},{4,0},{8,12},{12,8},{16,20},{20,16},{24,28},{28,24},{1,5},{5... | collective-permute-start | bytes 245768 | tf_op jit(solution)/shard_map/ppermute | solution.py:454
  62.2 1.5 %collective-permute-start.11 = (f32[2,40,256]{2,1,0:T(8,128)S(1)}, f32[2,40,256]{2,1,0:T(8,128)S(1)}, u32[]{:S(2)}, u32[]{:S(2)}) collective-permute-start(f32[2,40,256]{2,1,0:T(8,128)S(1)} %get-tuple-element.43), channel_id=1, source_target_pairs={{0,8},{4,12},{8,0},{12,4},{16,24},{20,28},{24,16},{28,20},{1,9},{5... | collective-permute-start | bytes 245768 | tf_op jit(solution)/shard_map/ppermute | solution.py:454
  63.8 2.9 %collective-permute-start.13 = (f32[2,40,256]{2,1,0:T(8,128)S(1)}, f32[2,40,256]{2,1,0:T(8,128)S(1)}, u32[]{:S(2)}, u32[]{:S(2)}) collective-permute-start(f32[2,40,256]{2,1,0:T(8,128)S(1)} %get-tuple-element.45), channel_id=1, source_target_pairs={{0,16},{4,20},{8,24},{12,28},{16,0},{20,4},{24,8},{28,12},{1,17},{... | collective-permute-start | bytes 245768 | tf_op jit(solution)/shard_map/ppermute | solution.py:454
  66.6 1.5 %collective-permute-start.14 = (f32[2,40,256]{2,1,0:T(8,128)S(1)}, f32[2,40,256]{2,1,0:T(8,128)S(1)}, u32[]{:S(2)}, u32[]{:S(2)}) collective-permute-start(f32[2,40,256]{2,1,0:T(8,128)S(1)} %get-tuple-element.46), channel_id=1, source_target_pairs={{0,20},{4,16},{8,28},{12,24},{16,4},{20,0},{24,12},{28,8},{1,21},{... | collective-permute-start | bytes 245768 | tf_op jit(solution)/shard_map/ppermute | solution.py:454
  68.1 3.3 %collective-permute-start.15 = (f32[2,40,256]{2,1,0:T(8,128)S(1)}, f32[2,40,256]{2,1,0:T(8,128)S(1)}, u32[]{:S(2)}, u32[]{:S(2)}) collective-permute-start(f32[2,40,256]{2,1,0:T(8,128)S(1)} %get-tuple-element.47), channel_id=1, source_target_pairs={{0,24},{4,28},{8,16},{12,20},{16,8},{20,12},{24,0},{28,4},{1,25},{... | collective-permute-start | bytes 245768 | tf_op jit(solution)/shard_map/ppermute | solution.py:454
  71.4 8.3 %collective-permute-done.14.refs_5_ = f32[2,40,256]{2,1,0:T(8,128)S(1)} collective-permute-done((f32[2,40,256]{2,1,0:T(8,128)S(1)}, f32[2,40,256]{2,1,0:T(8,128)S(1)}, u32[]{:S(2)}, u32[]{:S(2)}) %collective-permute-start.14) | collective-permute-done | bytes 81952 | tf_op jit(solution)/shard_map/ppermute | solution.py:454
  79.8 1.1 %assemble.1 = f32[2,512,256]{2,1,0:T(8,128)} custom-call(f32[8,2,24,256]{3,2,1,0:T(8,128)S(1)} %all-to-all-done.whole_ref, f32[2,40,256]{2,1,0:T(8,128)S(1)} %get-tuple-element.41.refs_0_, f32[2,40,256]{2,1,0:T(8,128)S(1)} %collective-permute-done.10.refs_1_, f32[2,40,256]{2,1,0:T(8,128)S(1)} %collective-permute-done.11.refs_2_, ...), custom_call_target="tpu_custom_call" | custom-call | tf_op jit(solution)/shard_map/assemble/pallas_call | solution.py:457
  (47 shorter events, 1.1 us)
Async XLA Ops:
  3.1 11.1 %copy-start.9 = (f32[144,128]{1,0:T(8,128)S(1)}, f32[144,128]{1,0:T(8,128)}, u32[]{:S(2)}) copy-start(f32[144,128]{1,0:T(8,128)} %get-tuple-element.32) | copy-start | bytes 221188
  3.1 13.9 %copy-start.8 = (f32[144,128]{1,0:T(8,128)S(1)}, f32[144,128]{1,0:T(8,128)}, u32[]{:S(2)}) copy-start(f32[144,128]{1,0:T(8,128)} %get-tuple-element.33) | copy-start | bytes 221188
  3.1 15.3 %copy-start.7 = (f32[144,128]{1,0:T(8,128)S(1)}, f32[144,128]{1,0:T(8,128)}, u32[]{:S(2)}) copy-start(f32[144,128]{1,0:T(8,128)} %get-tuple-element.34) | copy-start | bytes 221188
  3.1 19.1 %copy-start.6 = (f32[144,128]{1,0:T(8,128)S(1)}, f32[144,128]{1,0:T(8,128)}, u32[]{:S(2)}) copy-start(f32[144,128]{1,0:T(8,128)} %get-tuple-element.35) | copy-start | bytes 221188
  3.1 33.3 %copy-start = (f32[144,128]{1,0:T(8,128)S(1)}, f32[144,128]{1,0:T(8,128)}, u32[]{:S(2)}) copy-start(f32[144,128]{1,0:T(8,128)} %get-tuple-element.28.refs_0_) | copy-start | bytes 221188
  3.2 43.8 %all-to-all-start.1 = ((f32[8,2,32,256]{3,2,1,0:T(8,128)}), f32[8,2,32,256]{3,2,1,0:T(8,128)S(1)}, u32[]{:S(2)}, u32[]{:S(2)}) async-start(f32[8,2,32,256]{3,2,1,0:T(8,128)} %get-tuple-element.40), calls=%async_computation.1 | async-start | bytes 1048576 | tf_op jit(solution)/shard_map/all_to_all | solution.py:398
  10.6 7.9 %collective-permute-start = (f32[144,128]{1,0:T(8,128)S(1)}, f32[144,128]{1,0:T(8,128)S(1)}, u32[]{:S(2)}, u32[]{:S(2)}) collective-permute-start(f32[144,128]{1,0:T(8,128)S(1)} %copy-done.12), channel_id=1, source_target_pairs={{0,4},{4,0},{8,12},{12,8},{16,20},{20,16},{24,28},{28,24},{1,5},{5... | collective-permute-start | bytes 221192 | tf_op jit(solution)/shard_map/ppermute | solution.py:397
  12.6 9.6 %collective-permute-start.1 = (f32[144,128]{1,0:T(8,128)S(1)}, f32[144,128]{1,0:T(8,128)S(1)}, u32[]{:S(2)}, u32[]{:S(2)}) collective-permute-start(f32[144,128]{1,0:T(8,128)S(1)} %copy-done.11), channel_id=1, source_target_pairs={{0,8},{4,12},{8,0},{12,4},{16,24},{20,28},{24,16},{28,20},{1,9},{5... | collective-permute-start | bytes 221192 | tf_op jit(solution)/shard_map/ppermute | solution.py:397
  14.1 12.6 %collective-permute-start.2 = (f32[144,128]{1,0:T(8,128)S(1)}, f32[144,128]{1,0:T(8,128)S(1)}, u32[]{:S(2)}, u32[]{:S(2)}) collective-permute-start(f32[144,128]{1,0:T(8,128)S(1)} %copy-done.10), channel_id=1, source_target_pairs={{0,12},{4,8},{8,4},{12,0},{16,28},{20,24},{24,20},{28,16},{1,13},{... | collective-permute-start | bytes 221192 | tf_op jit(solution)/shard_map/ppermute | solution.py:397
  14.2 20.2 %collective-permute-start.3 = (f32[144,128]{1,0:T(8,128)S(1)}, f32[144,128]{1,0:T(8,128)S(1)}, u32[]{:S(2)}, u32[]{:S(2)}) collective-permute-start(f32[144,128]{1,0:T(8,128)S(1)} %copy-done.9), channel_id=1, source_target_pairs={{0,16},{4,20},{8,24},{12,28},{16,0},{20,4},{24,8},{28,12},{1,17},{... | collective-permute-start | bytes 221192 | tf_op jit(solution)/shard_map/ppermute | solution.py:397
  17.0 19.4 %collective-permute-start.4 = (f32[144,128]{1,0:T(8,128)S(1)}, f32[144,128]{1,0:T(8,128)S(1)}, u32[]{:S(2)}, u32[]{:S(2)}) collective-permute-start(f32[144,128]{1,0:T(8,128)S(1)} %copy-done.8), channel_id=1, source_target_pairs={{0,20},{4,16},{8,28},{12,24},{16,4},{20,0},{24,12},{28,8},{1,21},{... | collective-permute-start | bytes 221192 | tf_op jit(solution)/shard_map/ppermute | solution.py:397
  18.5 18.0 %collective-permute-start.5 = (f32[144,128]{1,0:T(8,128)S(1)}, f32[144,128]{1,0:T(8,128)S(1)}, u32[]{:S(2)}, u32[]{:S(2)}) collective-permute-start(f32[144,128]{1,0:T(8,128)S(1)} %copy-done.7), channel_id=1, source_target_pairs={{0,24},{4,28},{8,16},{12,20},{16,8},{20,12},{24,0},{28,4},{1,25},{... | collective-permute-start | bytes 221192 | tf_op jit(solution)/shard_map/ppermute | solution.py:397
  22.2 14.3 %collective-permute-start.6 = (f32[144,128]{1,0:T(8,128)S(1)}, f32[144,128]{1,0:T(8,128)S(1)}, u32[]{:S(2)}, u32[]{:S(2)}) collective-permute-start(f32[144,128]{1,0:T(8,128)S(1)} %copy-done.6), channel_id=1, source_target_pairs={{0,28},{4,24},{8,20},{12,16},{16,12},{20,8},{24,4},{28,0},{1,29},{... | collective-permute-start | bytes 221192 | tf_op jit(solution)/shard_map/ppermute | solution.py:397
  36.5 3.8 %collective-permute-start.9 = (f32[72,128]{1,0:T(8,128)S(1)}, f32[72,128]{1,0:T(8,128)S(1)}, u32[]{:S(2)}, u32[]{:S(2)}) collective-permute-start(f32[72,128]{1,0:T(8,128)S(1)} %merge.1.refs_0_), channel_id=1, source_target_pairs={{0,3},{1,2},{2,1},{3,0},{4,7},{5,6},{6,5},{7,4},{8,11},{9,10},{10,... | collective-permute-start | bytes 110600 | tf_op jit(solution)/shard_map/ppermute | solution.py:421
  36.6 4.2 %collective-permute-start.8 = (f32[72,128]{1,0:T(8,128)S(1)}, f32[72,128]{1,0:T(8,128)S(1)}, u32[]{:S(2)}, u32[]{:S(2)}) collective-permute-start(f32[72,128]{1,0:T(8,128)S(1)} %merge.1.refs_0_), channel_id=1, source_target_pairs={{0,2},{1,3},{2,0},{3,1},{4,6},{5,7},{6,4},{7,5},{8,10},{9,11},{10,... | collective-permute-start | bytes 110600 | tf_op jit(solution)/shard_map/ppermute | solution.py:421
  38.2 2.6 %collective-permute-start.7 = (f32[72,128]{1,0:T(8,128)S(1)}, f32[72,128]{1,0:T(8,128)S(1)}, u32[]{:S(2)}, u32[]{:S(2)}) collective-permute-start(f32[72,128]{1,0:T(8,128)S(1)} %merge.1.refs_0_), channel_id=1, source_target_pairs={{0,1},{1,0},{2,3},{3,2},{4,5},{5,4},{6,7},{7,6},{8,9},{9,8},{10,11... | collective-permute-start | bytes 110600 | tf_op jit(solution)/shard_map/ppermute | solution.py:421
  47.0 24.4 %all-to-all-start = ((f32[8,2,24,256]{3,2,1,0:T(8,128)}), f32[8,2,24,256]{3,2,1,0:T(8,128)S(1)}, u32[]{:S(2)}, u32[]{:S(2)}) async-start(f32[8,2,24,256]{3,2,1,0:T(8,128)} %bitcast.1), calls=%async_computation | async-start | bytes 786432 | tf_op jit(solution)/shard_map/all_to_all | solution.py:440
  60.1 7.9 %collective-permute-start.10 = (f32[2,40,256]{2,1,0:T(8,128)S(1)}, f32[2,40,256]{2,1,0:T(8,128)S(1)}, u32[]{:S(2)}, u32[]{:S(2)}) collective-permute-start(f32[2,40,256]{2,1,0:T(8,128)S(1)} %get-tuple-element.42), channel_id=1, source_target_pairs={{0,4},{4,0},{8,12},{12,8},{16,20},{20,16},{24,28},{28,24},{1,5},{5... | collective-permute-start | bytes 245768 | tf_op jit(solution)/shard_map/ppermute | solution.py:454
  62.2 9.1 %collective-permute-start.11 = (f32[2,40,256]{2,1,0:T(8,128)S(1)}, f32[2,40,256]{2,1,0:T(8,128)S(1)}, u32[]{:S(2)}, u32[]{:S(2)}) collective-permute-start(f32[2,40,256]{2,1,0:T(8,128)S(1)} %get-tuple-element.43), channel_id=1, source_target_pairs={{0,8},{4,12},{8,0},{12,4},{16,24},{20,28},{24,16},{28,20},{1,9},{5... | collective-permute-start | bytes 245768 | tf_op jit(solution)/shard_map/ppermute | solution.py:454
  63.7 7.7 %collective-permute-start.12 = (f32[2,40,256]{2,1,0:T(8,128)S(1)}, f32[2,40,256]{2,1,0:T(8,128)S(1)}, u32[]{:S(2)}, u32[]{:S(2)}) collective-permute-start(f32[2,40,256]{2,1,0:T(8,128)S(1)} %get-tuple-element.44), channel_id=1, source_target_pairs={{0,12},{4,8},{8,4},{12,0},{16,28},{20,24},{24,20},{28,16},{1,13},{... | collective-permute-start | bytes 245768 | tf_op jit(solution)/shard_map/ppermute | solution.py:454
  63.8 7.7 %collective-permute-start.13 = (f32[2,40,256]{2,1,0:T(8,128)S(1)}, f32[2,40,256]{2,1,0:T(8,128)S(1)}, u32[]{:S(2)}, u32[]{:S(2)}) collective-permute-start(f32[2,40,256]{2,1,0:T(8,128)S(1)} %get-tuple-element.45), channel_id=1, source_target_pairs={{0,16},{4,20},{8,24},{12,28},{16,0},{20,4},{24,8},{28,12},{1,17},{... | collective-permute-start | bytes 245768 | tf_op jit(solution)/shard_map/ppermute | solution.py:454
  66.6 13.1 %collective-permute-start.14 = (f32[2,40,256]{2,1,0:T(8,128)S(1)}, f32[2,40,256]{2,1,0:T(8,128)S(1)}, u32[]{:S(2)}, u32[]{:S(2)}) collective-permute-start(f32[2,40,256]{2,1,0:T(8,128)S(1)} %get-tuple-element.46), channel_id=1, source_target_pairs={{0,20},{4,16},{8,28},{12,24},{16,4},{20,0},{24,12},{28,8},{1,21},{... | collective-permute-start | bytes 245768 | tf_op jit(solution)/shard_map/ppermute | solution.py:454
  68.1 11.7 %collective-permute-start.15 = (f32[2,40,256]{2,1,0:T(8,128)S(1)}, f32[2,40,256]{2,1,0:T(8,128)S(1)}, u32[]{:S(2)}, u32[]{:S(2)}) collective-permute-start(f32[2,40,256]{2,1,0:T(8,128)S(1)} %get-tuple-element.47), channel_id=1, source_target_pairs={{0,24},{4,28},{8,16},{12,20},{16,8},{20,12},{24,0},{28,4},{1,25},{... | collective-permute-start | bytes 245768 | tf_op jit(solution)/shard_map/ppermute | solution.py:454
  71.4 8.4 %collective-permute-start.16 = (f32[2,40,256]{2,1,0:T(8,128)S(1)}, f32[2,40,256]{2,1,0:T(8,128)S(1)}, u32[]{:S(2)}, u32[]{:S(2)}) collective-permute-start(f32[2,40,256]{2,1,0:T(8,128)S(1)} %get-tuple-element.48), channel_id=1, source_target_pairs={{0,28},{4,24},{8,20},{12,16},{16,12},{20,8},{24,4},{28,0},{1,29},{... | collective-permute-start | bytes 245768 | tf_op jit(solution)/shard_map/ppermute | solution.py:454
  (8 other events, 44.9 us)
